TPU v7x, 256 devices: a whole 4x4x8 slice. The times are simulated.
256 devices in a mesh: pair: 32 (over z, x), occ: 8 (over y, core).
Axes of the slice: x: 4, y: 4, z: 8, core: 2. Of those that a mesh axis runs over, the one named last changes fastest.
Arguments:
- integrals: bfloat16 [32, 256, 64, 1024], P('pair', None, None, 'occ'), may hold values from -6 to 6
- occ_coeffs: bfloat16 [6144, 128], replicated, may hold values from -0.125 to 0.125
- virt_coeffs: bfloat16 [6144, 5120], P(None, 'pair'), may hold values from -0.078125 to 0.078125
- block_ids: int32 [2, 32, 256], P(None, 'pair'), may hold values from 0 to 95, as said below
- live_mask: int32 [32, 256], P('pair'), may hold values from 0 to 1, as said below
Outputs:
- factors: bfloat16 [128, 16, 5120], P('occ', None, 'pair')
Inputs may be any that keep to these rules, and one draw needn't show every extreme that they name: `block_ids`: slot s of pair index p holds a nu block N with N // 3 == s // 8; each (mu block, nu block) pair is held by at most one slot of all pair indices. `live_mask`: among the 8 slots s with the same s // 8 of one pair index, at most 4 are 1, and exactly 4 for some such group of every pair index.
All inputs are finite; a program needn't handle non-finite values.
Results may differ from a plain program's by a relative error of at most 0.017.
Values may be sent and summed in bfloat16 or wider, within the bound.
A program may use at most 64 MiB of HBM per device.

v0:
```python
import jax
import jax.numpy as jnp
from jax import lax
from jax.sharding import PartitionSpec as P

LIVE = 4


def in_one_piece(arrays, axis, split_dim, concat_dim, along):
    both = jnp.concatenate(arrays, axis=along)
    filled, at, done = (
        lax.all_to_all(both, axis, split_axis=split_dim, concat_axis=concat_dim, tiled=True),
        0,
        [],
    )
    for a in arrays:
        done.append(lax.slice_in_dim(filled, at, at + a.shape[along], axis=along))
        at += a.shape[along]
    return tuple(done)


def half_transform(block_data, mu_index, coeff_blocks):
    slot_count, block_width = (block_data.shape[0], block_data.shape[1])
    aux_local = block_data.shape[2] // block_width
    coeff_rows = jnp.take(coeff_blocks, mu_index, axis=0)
    shaped = block_data.reshape(slot_count, block_width, aux_local, block_width)
    return jnp.einsum("snqm,smi->snqi", shaped, coeff_rows, preferred_element_type=jnp.float32)


def on_device(integrals, occ_coeffs, virt_coeffs, block_ids, live_mask):
    blocks = integrals[0]
    slot_count, block_width = (blocks.shape[0], blocks.shape[1])
    aux_local = blocks.shape[2] // block_width
    occ_count = occ_coeffs.shape[1]
    block_count = occ_coeffs.shape[0] // block_width
    owners = lax.axis_size("pair")
    owned_count = block_count // owners
    group_size = slot_count // owners
    coeff_blocks = occ_coeffs.reshape(block_count, block_width, occ_count)
    mu_index = block_ids[0, 0]
    nu_index = block_ids[1, 0]
    live_flags = live_mask[0]
    grouped_live = live_flags.reshape(owners, group_size)
    sort_keys = (1 - grouped_live) * group_size + jnp.arange(group_size)[None, :]
    chosen = jnp.argsort(sort_keys, axis=1)[:, :LIVE]
    valid_flags = jnp.take_along_axis(grouped_live, chosen, axis=1).reshape(-1)
    slot_index = (chosen + jnp.arange(owners)[:, None] * group_size).reshape(-1)
    send_blocks = blocks[slot_index] * valid_flags[:, None, None].astype(jnp.bfloat16)
    send_blocks = send_blocks.reshape(owners, LIVE, block_width, aux_local * block_width)
    send_mu = mu_index[slot_index].reshape(owners, LIVE)
    send_nu = nu_index[slot_index].reshape(owners, LIVE)
    got_blocks, got_mu, got_nu = (
        lax.all_to_all(send_blocks, "pair", split_axis=0, concat_axis=0, tiled=True),
        *in_one_piece((send_mu, send_nu), "pair", 0, 0, 1),
    )
    partial_terms = half_transform(
        got_blocks.reshape(owners * LIVE, block_width, -1), got_mu.reshape(-1), coeff_blocks
    )
    selector = got_nu.reshape(-1)[None, :] % owned_count == jnp.arange(owned_count)[:, None]
    summed = jnp.dot(
        selector.astype(jnp.float32),
        partial_terms.reshape(owners * LIVE, -1),
        precision=lax.Precision.HIGHEST,
    )
    summed = summed.reshape(owned_count, block_width, aux_local, occ_count)
    half_sums = summed.astype(jnp.bfloat16)
    slab_sums = lax.all_to_all(half_sums, "occ", split_axis=3, concat_axis=2, tiled=True)
    aux_count, slab_rows = (slab_sums.shape[2], slab_sums.shape[3])
    shard_piece = lax.all_gather(slab_sums, "pair", axis=0, tiled=True)
    piece_blocks = shard_piece.shape[0]
    flat_piece = shard_piece.reshape(piece_blocks * block_width, aux_count, slab_rows)
    result = jnp.einsum("nqi,na->iqa", flat_piece, virt_coeffs, preferred_element_type=jnp.float32)
    return result.astype(jnp.bfloat16)


def solution(mesh):
    return jax.shard_map(
        on_device,
        mesh=mesh,
        in_specs=(
            P("pair", None, None, "occ"),
            P(),
            P(None, "pair"),
            P(None, "pair", None),
            P("pair", None),
        ),
        out_specs=P("occ", None, "pair"),
        check_vma=False,
    )
```

profile of v0, /device:TPU:1, one launch (start us, length us, event | category | flops | bytes accessed | tf_op | source)
XLA Modules:
  0.0 251.1 jit_solution(16702428918213110654)
XLA Ops:
  6.5 0.8 fusion.25
  7.9 1.3 reduce.3
  10.3 1.3 gather_fusion.4
  12.0 1.3 gather_fusion.1
  13.2 1.3 gather_fusion
  15.4 11.9 %all-to-all-start = ((s32[32,1,8]{2,1,0:T(1,128)}), s32[32,1,8]{2,1,0:T(1,128)S(1)}, u32[]{:S(2)}, u32[]{:S(2)}) async-start(s32[32,1,8]{2,1,0:T(1,128)} %bitcast.4), calls=%async_computation | async-start | bytes 32768 | tf_op jit(solution)/shard_map/all_to_all | solution.py:12
  27.4 4.3 %gather_fusion.2 = bf16[128,64,128]{2,1,0:T(8,128)(2,1)} fusion(bf16[256,64,128]{2,1,0:T(8,128)(2,1)} %bitcast.62, s32[1024]{0:T(1024)S(1)} %pad_clamp_fusion.1), kind=kCustom, calls=%fused_computation.2 | custom fusion | bytes 4194816 | tf_op jit(solution)/shard_map/gather | solution.py:48
  31.7 3.1 %broadcast_multiply_fusion = bf16[32,4,64,128]{3,2,1,0:T(8,128)(2,1)} fusion(bf16[32,4,64,128]{3,2,1,0:T(8,128)(2,1)} %bitcast.60, bf16[32,4]{1,0:T(8,128)(2,1)S(1)} %copy.55), kind=kLoop, calls=%fused_computation.18 | loop fusion | flops 1048576 | bytes 4194560 | tf_op jit(solution)/shard_map/mul | solution.py:48
  34.8 1.0 all-to-all-done
  35.8 8.5 %all-to-all-start.1 = ((bf16[32,4,64,128]{3,2,1,0:T(8,128)(2,1)}), bf16[32,4,64,128]{3,2,1,0:T(8,128)(2,1)}, u32[]{:S(2)}, u32[]{:S(2)}) async-start(bf16[32,4,64,128]{3,2,1,0:T(8,128)(2,1)} %broadcast_multiply_fusion), calls=%async_computation.1 | async-start | bytes 4194304 | tf_op jit(solution)/shard_map/all_to_all | solution.py:53
  45.1 0.8 reshape.144
  45.9 0.8 reshape.142
  46.7 0.8 rem.20
  47.6 2.2 gather_fusion.3
  49.7 42.5 %all-to-all-done.1 = bf16[32,4,64,128]{3,2,1,0:T(8,128)(2,1)} async-done(((bf16[32,4,64,128]{3,2,1,0:T(8,128)(2,1)}), bf16[32,4,64,128]{3,2,1,0:T(8,128)(2,1)}, u32[]{:S(2)}, u32[]{:S(2)}) %all-to-all-start.1) | async-done | bytes 2097184 | tf_op jit(solution)/shard_map/all_to_all | solution.py:53
  92.3 8.2 %reshape_reshape.3 = bf16[128,64,2,64]{3,2,1,0:T(2,128)(2,1)} reshape(bf16[32,4,64,128]{3,2,1,0:T(8,128)(2,1)} %all-to-all-done.1) | data formatting | bytes 4194304 | tf_op jit(solution)/shard_map/reshape;reshape | solution.py:26
  100.5 7.4 %fusion.2 = f32[128,64,2,128]{3,1,2,0:T(8,128)} fusion(bf16[128,64,2,64]{3,2,1,0:T(2,128)(2,1)} %reshape_reshape.3, bf16[128,64,128]{2,1,0:T(8,128)(2,1)} %gather_fusion.3, pred[128]{0:T(512)(128)(4,1)S(1)} %compare_and_fusion), kind=kOutput, calls=%fused_computation.7 | convolution fusion | flops 269484032 | bytes 12583040 | tf_op jit(solution)/shard_map/snqm,smi->snqi/dot_general | solution.py:27
  107.9 9.2 %copy.57 = f32[128,64,2,128]{0,3,2,1:T(8,128)} copy(f32[128,64,2,128]{3,1,2,0:T(8,128)} %fusion.2) | data formatting | bytes 16777216 | tf_op jit(solution)/shard_map/snqm,smi->snqi/dot_general | solution.py:27
  117.1 7.1 %fusion.12 = bf16[3,64,2,128]{3,0,2,1:T(4,128)(2,1)S(1)} fusion(f32[128,64,2,128]{0,3,2,1:T(8,128)} %copy.57, s32[128]{0:T(128)S(1)} %and_select_fusion), kind=kOutput, calls=%fused_computation.15 | convolution fusion | flops 75547008 | bytes 8487424 | tf_op jit(solution)/shard_map/dot_general | solution.py:60
  124.6 12.4 %all_to_all.35 = bf16[8,2,3072]{2,1,0:T(2,128)(2,1)S(1)} all-to-all(bf16[8,2,3072]{2,1,0:T(2,128)(2,1)S(1)} %reshape.202), channel_id=1, replica_groups=mesh['pair'=32,'occ'=8] {'occ'}, dimensions={0} | all-to-all | bytes 196608 | tf_op jit(solution)/shard_map/all_to_all | solution.py:67
  137.9 84.2 %all-gather.2.cloned.1.call-done = bf16[96,64,16,16]{1,3,2,0:T(8,128)(2,1)} async-done(((bf16[3,64,16,16]{1,3,2,0:T(8,128)(2,1)}), bf16[96,64,16,16]{1,3,2,0:T(8,128)(2,1)}) %all-gather.2.cloned.1.call-update) | async-done | bytes 3145744 | tf_op jit(solution)/shard_map/all_gather | solution.py:69
  222.1 9.5 %copy.61 = bf16[96,64,16,16]{1,0,3,2:T(8,128)(2,1)} copy(bf16[96,64,16,16]{1,3,2,0:T(8,128)(2,1)} %all-gather.2.cloned.1.call-done) | data formatting | bytes 6291456 | tf_op jit(solution)/shard_map/all_gather | solution.py:69
  231.6 9.1 %reshape.146 = bf16[6144,16,16]{0,2,1:T(8,128)(2,1)} reshape(bf16[96,64,16,16]{1,0,3,2:T(8,128)(2,1)} %copy.61) | data formatting | bytes 6291456 | tf_op jit(solution)/shard_map/reshape | solution.py:71
  240.7 2.9 %fusion.15 = bf16[16,16,160]{2,0,1:T(8,128)(2,1)S(1)} fusion(bf16[6144,16,16]{0,2,1:T(8,128)(2,1)} %reshape.146, bf16[6144,160]{0,1:T(8,128)(2,1)S(1)} %copy-done), kind=kOutput, calls=%fused_computation.16 | convolution fusion | flops 503357440 | bytes 5193728 | tf_op jit(solution)/shard_map/nqi,na->iqa/dot_general | solution.py:72
  (38 shorter events, 5.6 us)
Async XLA Ops:
  6.5 234.1 %copy-start = (bf16[6144,160]{0,1:T(8,128)(2,1)S(1)}, bf16[6144,160]{0,1:T(8,128)(2,1)}, u32[]{:S(2)}) copy-start(bf16[6144,160]{0,1:T(8,128)(2,1)} %param.7) | copy-start | bytes 5898244
  15.4 20.4 %all-to-all-start = ((s32[32,1,8]{2,1,0:T(1,128)}), s32[32,1,8]{2,1,0:T(1,128)S(1)}, u32[]{:S(2)}, u32[]{:S(2)}) async-start(s32[32,1,8]{2,1,0:T(1,128)} %bitcast.4), calls=%async_computation | async-start | bytes 32768 | tf_op jit(solution)/shard_map/all_to_all | solution.py:12
  34.8 12.7 %copy-start.1 = (bf16[6144,128]{1,0:T(8,128)(2,1)S(1)}, bf16[6144,128]{1,0:T(8,128)(2,1)}, u32[]{:S(2)}) copy-start(bf16[6144,128]{1,0:T(8,128)(2,1)} %param.6) | copy-start | bytes 4718596
  35.8 56.5 %all-to-all-start.1 = ((bf16[32,4,64,128]{3,2,1,0:T(8,128)(2,1)}), bf16[32,4,64,128]{3,2,1,0:T(8,128)(2,1)}, u32[]{:S(2)}, u32[]{:S(2)}) async-start(bf16[32,4,64,128]{3,2,1,0:T(8,128)(2,1)} %broadcast_multiply_fusion), calls=%async_computation.1 | async-start | bytes 4194304 | tf_op jit(solution)/shard_map/all_to_all | solution.py:53
  44.3 177.8 %all-gather.2.cloned.1.call-start = ((), (), s32[]{:S(2)}) async-start(), calls=%async_computation.3 | async-start | bytes 6488064 | tf_op jit(solution)/shard_map/all_gather | solution.py:69
Sparse Core Ops, SparseCore 0:
  138.0 84.0 all-gather.1
where the time goes:
time: 252 us; the launch traced here: 251 us
  waiting for transfers between devices  128 us (51%)
  local copies, waits for them, and re-layouts  53.1 us (21%)
  starting transfers between devices  20.4 us (8%)
  matrix products  17.4 us (7%)
  between operations  13.6 us (5%)
  blocking collectives  12.4 us (5%)
  other arithmetic  6.55 us (3%)
    all_gather x1, waiting for transfers between devices, on_device(): shard_piece = lax.all_gather(slab_sums, 'pair', axis=0, tiled=True)  84.2 us
    all_to_all x1, waiting for transfers between devices, on_device(): lax.all_to_all(send_blocks, 'pair', split_axis=0, concat_axis=0, tiled=True)  42.5 us
    all_to_all x1, blocking collectives, on_device(): lax.all_to_all(half_sums, 'occ', split_axis=3, concat_axis=2, tiled=True)  12.4 us
    all_to_all x1, starting transfers between devices, in_one_piece(): lax.all_to_all(both, axis, split_axis=split_dim, concat_axis=concat_dim,...  11.9 us
    all_gather x1, local copies, waits for them, and re-layouts, on_device(): shard_piece = lax.all_gather(slab_sums, 'pair', axis=0, tiled=True)  9.49 us
    dot_general x1, local copies, waits for them, and re-layouts, half_transform(): jnp.einsum('snqm,smi->snqi', shaped, coeff_rows, preferred_element_type=j...  9.2 us
    reshape x1, local copies, waits for them, and re-layouts, on_device(): shard_piece.reshape(piece_blocks * block_width, aux_count, slab_rows)  9.09 us
    all_to_all x1, starting transfers between devices, on_device(): lax.all_to_all(send_blocks, 'pair', split_axis=0, concat_axis=0, tiled=True)  8.52 us
  transfers between devices with their start and end apart: 3, of which 3 were waited for; matrix products, arithmetic and copies ran while one was open for 5% of the time, Pallas kernels for 0%

commit v1 on v0

--- a/solution.py
+++ b/solution.py
@@ -66,7 +66,9 @@
     half_sums = summed.astype(jnp.bfloat16)
     slab_sums = lax.all_to_all(half_sums, "occ", split_axis=3, concat_axis=2, tiled=True)
     aux_count, slab_rows = (slab_sums.shape[2], slab_sums.shape[3])
-    shard_piece = lax.all_gather(slab_sums, "pair", axis=0, tiled=True)
+    shard_piece = jnp.concatenate(
+        lax.all_to_all(jnp.stack([slab_sums] * lax.axis_size("pair")), "pair", 0, 0), axis=0
+    )
     piece_blocks = shard_piece.shape[0]
     flat_piece = shard_piece.reshape(piece_blocks * block_width, aux_count, slab_rows)
     result = jnp.einsum("nqi,na->iqa", flat_piece, virt_coeffs, preferred_element_type=jnp.float32)

time: 252 us -> 262 us (1.040); the launches traced: 251 us -> 258 us
  waiting for transfers between devices: 128 us -> 43.5 us
  blocking collectives: 12.4 us -> 89.2 us
  local copies, waits for them, and re-layouts: 53.1 us -> 81.1 us
  between operations: 13.6 us -> 0.18 us
    all_gather x1 -> x0, waiting for transfers between devices: 84.2 us -> none  [on_device(): shard_piece = lax.all_gather(slab_sums, 'pair', axis=0, tiled=True)]
    all_to_all x0 -> x1, blocking collectives: none -> 76.7 us  [on_device(): lax.all_to_all(jnp.stack([slab_sums] * lax.axis_size('pair')), 'pair', 0, 0)]
    unnamed x7 -> x10, local copies, waits for them, and re-layouts: 0.86 us -> 22.7 us
    another operation x0 -> x1, local copies, waits for them, and re-layouts: none -> 14.1 us  [on_device(): shard_piece.reshape(piece_blocks * block_width, aux_count, slab_rows)]
    all_to_all x0 -> x1, local copies, waits for them, and re-layouts: none -> 11.4 us  [on_device(): lax.all_to_all(jnp.stack([slab_sums] * lax.axis_size('pair')), 'pair', 0, 0)]
    all_gather x1 -> x0, local copies, waits for them, and re-layouts: 9.49 us -> none  [on_device(): shard_piece = lax.all_gather(slab_sums, 'pair', axis=0, tiled=True)]
    reshape x1 -> x0, local copies, waits for them, and re-layouts: 9.09 us -> none  [on_device(): shard_piece.reshape(piece_blocks * block_width, aux_count, slab_rows)]
  transfers between devices with their start and end apart: 3 -> 2, of which waited for: 3 -> 2; matrix products, arithmetic and copies ran while one was open for 5% -> 5% of each run, Pallas kernels for 0% -> 0%
where the time goes in v1:
time: 262 us; the launch traced here: 258 us
  blocking collectives  89.2 us (34%)
  local copies, waits for them, and re-layouts  81.1 us (31%)
  waiting for transfers between devices  43.5 us (17%)
  starting transfers between devices  20.4 us (8%)
  matrix products  17.4 us (7%)
  other arithmetic  6.54 us (2%)
    all_to_all x1, blocking collectives, on_device(): lax.all_to_all(jnp.stack([slab_sums] * lax.axis_size('pair')), 'pair', 0, 0)  76.7 us
    all_to_all x1, waiting for transfers between devices, on_device(): lax.all_to_all(send_blocks, 'pair', split_axis=0, concat_axis=0, tiled=True)  42.5 us
    unnamed x10, local copies, waits for them, and re-layouts  22.7 us
    another operation x1, local copies, waits for them, and re-layouts, on_device(): shard_piece.reshape(piece_blocks * block_width, aux_count, slab_rows)  14.1 us
    all_to_all x1, blocking collectives, on_device(): lax.all_to_all(half_sums, 'occ', split_axis=3, concat_axis=2, tiled=True)  12.4 us
    all_to_all x1, starting transfers between devices, in_one_piece(): lax.all_to_all(both, axis, split_axis=split_dim, concat_axis=concat_dim,...  11.9 us
    all_to_all x1, local copies, waits for them, and re-layouts, on_device(): lax.all_to_all(jnp.stack([slab_sums] * lax.axis_size('pair')), 'pair', 0, 0)  11.4 us
    dot_general x1, local copies, waits for them, and re-layouts, half_transform(): jnp.einsum('snqm,smi->snqi', shaped, coeff_rows, preferred_element_type=j...  9.17 us
  transfers between devices with their start and end apart: 2, of which 2 were waited for; matrix products, arithmetic and copies ran while one was open for 5% of the time, Pallas kernels for 0%

profile of v1, /device:TPU:1, one launch (start us, length us, event | category | flops | bytes accessed | tf_op | source)
XLA Modules:
  0.0 258.3 jit_solution(2381215507269856049)
XLA Ops:
  0.0 0.8 fusion.25
  1.4 1.3 reduce.3
  3.7 1.3 gather_fusion.4
  5.4 1.3 gather_fusion.1
  6.7 1.3 gather_fusion
  8.9 11.9 %all-to-all-start = ((s32[32,1,8]{2,1,0:T(1,128)}), s32[32,1,8]{2,1,0:T(1,128)S(1)}, u32[]{:S(2)}, u32[]{:S(2)}) async-start(s32[32,1,8]{2,1,0:T(1,128)} %bitcast.4), calls=%async_computation | async-start | bytes 32768 | tf_op jit(solution)/shard_map/all_to_all | solution.py:12
  20.9 4.4 %gather_fusion.2 = bf16[128,64,128]{2,1,0:T(8,128)(2,1)} fusion(bf16[256,64,128]{2,1,0:T(8,128)(2,1)} %bitcast.64, s32[1024]{0:T(1024)S(1)} %pad_clamp_fusion.1), kind=kCustom, calls=%fused_computation.2 | custom fusion | bytes 4194816 | tf_op jit(solution)/shard_map/gather | solution.py:48
  25.2 3.1 %broadcast_multiply_fusion = bf16[32,4,64,128]{3,2,1,0:T(8,128)(2,1)} fusion(bf16[32,4,64,128]{3,2,1,0:T(8,128)(2,1)} %bitcast.62, bf16[32,4]{1,0:T(8,128)(2,1)S(1)} %copy.55), kind=kLoop, calls=%fused_computation.18 | loop fusion | flops 1048576 | bytes 4194560 | tf_op jit(solution)/shard_map/mul | solution.py:48
  28.3 1.0 all-to-all-done
  29.3 8.5 %all-to-all-start.1 = ((bf16[32,4,64,128]{3,2,1,0:T(8,128)(2,1)}), bf16[32,4,64,128]{3,2,1,0:T(8,128)(2,1)}, u32[]{:S(2)}, u32[]{:S(2)}) async-start(bf16[32,4,64,128]{3,2,1,0:T(8,128)(2,1)} %broadcast_multiply_fusion), calls=%async_computation.1 | async-start | bytes 4194304 | tf_op jit(solution)/shard_map/all_to_all | solution.py:53
  41.0 2.2 gather_fusion.3
  43.2 42.5 %all-to-all-done.1 = bf16[32,4,64,128]{3,2,1,0:T(8,128)(2,1)} async-done(((bf16[32,4,64,128]{3,2,1,0:T(8,128)(2,1)}), bf16[32,4,64,128]{3,2,1,0:T(8,128)(2,1)}, u32[]{:S(2)}, u32[]{:S(2)}) %all-to-all-start.1) | async-done | bytes 2097184 | tf_op jit(solution)/shard_map/all_to_all | solution.py:53
  85.7 8.2 %reshape_reshape.6 = bf16[128,64,2,64]{3,2,1,0:T(2,128)(2,1)} reshape(bf16[32,4,64,128]{3,2,1,0:T(8,128)(2,1)} %all-to-all-done.1) | data formatting | bytes 4194304 | tf_op jit(solution)/shard_map/reshape;reshape | solution.py:26
  93.9 7.4 %fusion.2 = f32[128,64,2,128]{3,1,2,0:T(8,128)} fusion(bf16[128,64,2,64]{3,2,1,0:T(2,128)(2,1)} %reshape_reshape.6, bf16[128,64,128]{2,1,0:T(8,128)(2,1)} %gather_fusion.3, pred[128]{0:T(512)(128)(4,1)S(1)} %compare_and_fusion), kind=kOutput, calls=%fused_computation.7 | convolution fusion | flops 269484032 | bytes 12583040 | tf_op jit(solution)/shard_map/snqm,smi->snqi/dot_general | solution.py:27
  101.3 9.2 %copy.57 = f32[128,64,2,128]{0,3,2,1:T(8,128)} copy(f32[128,64,2,128]{3,1,2,0:T(8,128)} %fusion.2) | data formatting | bytes 16777216 | tf_op jit(solution)/shard_map/snqm,smi->snqi/dot_general | solution.py:27
  110.5 7.1 %fusion.12 = bf16[3,64,2,128]{3,0,2,1:T(4,128)(2,1)S(1)} fusion(f32[128,64,2,128]{0,3,2,1:T(8,128)} %copy.57, s32[128]{0:T(128)S(1)} %and_select_fusion), kind=kOutput, calls=%fused_computation.15 | convolution fusion | flops 75547008 | bytes 8487424 | tf_op jit(solution)/shard_map/dot_general | solution.py:60
  118.0 12.4 %all_to_all.37 = bf16[8,2,3072]{2,1,0:T(2,128)(2,1)S(1)} all-to-all(bf16[8,2,3072]{2,1,0:T(2,128)(2,1)S(1)} %reshape.201), channel_id=1, replica_groups=mesh['pair'=32,'occ'=8] {'occ'}, dimensions={0} | all-to-all | bytes 196608 | tf_op jit(solution)/shard_map/all_to_all | solution.py:67
  130.7 4.2 %broadcast_bitcast_fusion = bf16[32,3,16,16,64]{4,3,2,1,0:T(8,128)(2,1)} fusion(bf16[3,64,16,16]{1,3,2,0:T(8,128)(2,1)S(1)} %bitcast.65), kind=kLoop, calls=%fused_computation.41 | loop fusion | bytes 3244032
  134.9 8.8 %reshape.203 = bf16[32,2,24576]{2,1,0:T(2,128)(2,1)} reshape(bf16[32,3,16,16,64]{4,3,2,1,0:T(8,128)(2,1)} %broadcast_bitcast_fusion) | data formatting | bytes 6291456
  143.7 76.7 %all_to_all.38 = bf16[32,2,24576]{2,1,0:T(2,128)(2,1)} all-to-all(bf16[32,2,24576]{2,1,0:T(2,128)(2,1)} %reshape.203), channel_id=1, replica_groups=mesh['pair'=32,'occ'=8] {'pair'}, dimensions={0} | all-to-all | bytes 6291456 | tf_op jit(solution)/shard_map/all_to_all | solution.py:70
  220.4 8.8 %reshape.204 = bf16[32,3,16,16,64]{4,3,2,1,0:T(8,128)(2,1)} reshape(bf16[32,2,24576]{2,1,0:T(2,128)(2,1)} %all_to_all.38) | data formatting | bytes 6291456
  229.2 11.4 %copy.61 = bf16[32,3,64,16,16]{2,1,0,4,3:T(4,128)(2,1)} copy(bf16[32,3,64,16,16]{2,4,3,1,0:T(8,128)(2,1)} %bitcast.61) | data formatting | bytes 6291456 | tf_op jit(solution)/shard_map/all_to_all | solution.py:70
  240.6 14.1 %reshape_reshape.7 = bf16[6144,16,16]{0,2,1:T(8,128)(2,1)} reshape(bf16[32,3,64,16,16]{2,1,0,4,3:T(4,128)(2,1)} %copy.61) | data formatting | bytes 6291456 | tf_op jit(solution)/shard_map/reshape;reshape | solution.py:73
  254.7 2.9 %fusion.15 = bf16[16,16,160]{2,0,1:T(8,128)(2,1)S(1)} fusion(bf16[6144,16,16]{0,2,1:T(8,128)(2,1)} %reshape_reshape.7, bf16[6144,160]{0,1:T(8,128)(2,1)S(1)} %copy-done), kind=kOutput, calls=%fused_computation.16 | convolution fusion | flops 503357440 | bytes 5193728 | tf_op jit(solution)/shard_map/nqi,na->iqa/dot_general | solution.py:74
  (39 shorter events, 7.4 us)
Async XLA Ops:
  0.0 254.7 %copy-start = (bf16[6144,160]{0,1:T(8,128)(2,1)S(1)}, bf16[6144,160]{0,1:T(8,128)(2,1)}, u32[]{:S(2)}) copy-start(bf16[6144,160]{0,1:T(8,128)(2,1)} %param.7) | copy-start | bytes 5898244
  8.9 20.4 %all-to-all-start = ((s32[32,1,8]{2,1,0:T(1,128)}), s32[32,1,8]{2,1,0:T(1,128)S(1)}, u32[]{:S(2)}, u32[]{:S(2)}) async-start(s32[32,1,8]{2,1,0:T(1,128)} %bitcast.4), calls=%async_computation | async-start | bytes 32768 | tf_op jit(solution)/shard_map/all_to_all | solution.py:12
  28.3 12.7 %copy-start.1 = (bf16[6144,128]{1,0:T(8,128)(2,1)S(1)}, bf16[6144,128]{1,0:T(8,128)(2,1)}, u32[]{:S(2)}) copy-start(bf16[6144,128]{1,0:T(8,128)(2,1)} %param.6) | copy-start | bytes 4718596
  29.3 56.5 %all-to-all-start.1 = ((bf16[32,4,64,128]{3,2,1,0:T(8,128)(2,1)}), bf16[32,4,64,128]{3,2,1,0:T(8,128)(2,1)}, u32[]{:S(2)}, u32[]{:S(2)}) async-start(bf16[32,4,64,128]{3,2,1,0:T(8,128)(2,1)} %broadcast_multiply_fusion), calls=%async_computation.1 | async-start | bytes 4194304 | tf_op jit(solution)/shard_map/all_to_all | solution.py:53
